TPU v7x, 256 devices: a whole 4x4x8 slice. The times are simulated.
256 devices in a mesh: basis: 4 (over x_lo, core), tm: 64 (over y, x_hi, z).
Axes of the slice: x: 4 (x_hi: 2, x_lo: 2; x = x_hi * 2 + x_lo), y: 4, z: 8, core: 2. Of those that a mesh axis runs over, the one named last changes fastest.
Arguments:
- strain: bfloat16 [3, 32768], P(None, 'tm'), may hold values from -6 to 6
- basis_filters: bfloat16 [4096, 2048], P('basis'), may hold values from -0.125 to 0.125
- coefficients: bfloat16 [8192, 4096], P(('basis', 'tm')), may hold values from -0.375 to 0.375
Outputs:
- snr: bfloat16 [8192, 3, 8192], P('basis', None, 'tm')
All inputs are finite; a program needn't handle non-finite values.
Results may differ from a plain program's by a relative error of at most 0.0049.
Values may be sent and summed in bfloat16 or wider, within the bound.
A program may use at most 128 MiB of HBM per device.

v0:
```python
import jax
import jax.numpy as jnp
from jax import lax
from jax.experimental import pallas as pl
from jax.experimental.pallas import tpu as pltpu
from jax.sharding import PartitionSpec as P

MESH = pl.DeviceIdType.MESH
STRIDE = 4
NZ, NY = 8, 4
LANES = 128
BF, F32 = jnp.bfloat16, jnp.float32


def kernel(
    s_ref, f_hbm, a_hbm, out_ref,
    a_all, s1, s_all, filt, hank, expand, corr, c1s, c1r, own, c2s, c2r, done,
    local_sem, s1_send, s1_recv, s2_send, s2_recv, row_send, row_recv,
    ring_send, ring_recv, c1_send, c1_recv, c2_send, c2_recv, c3_send, c3_recv, keep_sem,
):
    i = lax.axis_index("basis")
    j = lax.axis_index("tm")
    xl, core = i // 2, i % 2
    e, z = j // NZ, j % NZ
    y, xh = e // 2, e % 2
    rows = a_hbm.shape[0]
    depth = a_hbm.shape[1] // 4
    taps = f_hbm.shape[1]

    def flip(bit, by):
        return 1 - bit if by else bit

    def at(xl_, core_, y_, xh_, z_):
        return {"basis": xl_ * 2 + core_, "tm": (y_ * 2 + xh_) * NZ + z_}

    def remote(src, dst, send, recv, where):
        return pltpu.make_async_remote_copy(
            src_ref=src, dst_ref=dst, send_sem=send, recv_sem=recv,
            device_id=where, device_id_type=MESH,
        )

    peers = []
    for k in range(4):
        for dc in range(2):
            if k or dc:
                peers.append(at(flip(xl, k & 1), flip(core, dc), y, flip(xh, k >> 1), z))
    for dy in range(1, NY):
        for dx in range(2):
            peers.append(at(xl, core, (y + dy) % NY, flip(xh, dx), z))
    for dz in range(1, NZ):
        peers.append(at(xl, core, y, xh, (z + dz) % NZ))
    barrier = pltpu.get_barrier_semaphore()
    for where in peers:
        pl.semaphore_signal(barrier, inc=1, device_id=where, device_id_type=MESH)

    load_f = pltpu.make_async_copy(f_hbm, filt, local_sem.at[0])
    load_f.start()
    keep_a = pltpu.make_async_copy(
        a_hbm.at[:, pl.ds(pl.multiple_of(i * depth, LANES), depth)], a_all.at[z, 0, core], local_sem.at[1]
    )
    keep_a.start()
    keep_s = pltpu.make_async_copy(s_ref, s1.at[e], local_sem.at[2])
    keep_s.start()
    s_all[:, 2 * NY] = jnp.zeros((NZ,) + s_ref.shape, BF)
    pl.semaphore_wait(barrier, len(peers))

    pending = []
    for dy in range(NY):
        for dx in range(2):
            if dy or dx:
                c = remote(s_ref, s1.at[e], s1_send.at[dy * 2 + dx], s1_recv.at[dy * 2 + dx],
                           at(xl, core, (y + dy) % NY, flip(xh, dx), z))
                c.start()
                pending.append(c)
    for k in range(4):
        for dc in range(2):
            if k or dc:
                txl, tcore, txh = flip(xl, k & 1), flip(core, dc), flip(xh, k >> 1)
                c = remote(
                    a_hbm.at[:, pl.ds(pl.multiple_of((txl * 2 + tcore) * depth, LANES), depth)],
                    a_all.at[z, k, core], row_send.at[k * 2 + dc], row_recv.at[k * 2 + dc],
                    at(txl, tcore, y, txh, z))
                c.start()
                pending.append(c)
    keep_s.wait()
    for dy in range(NY):
        for dx in range(2):
            if dy or dx:
                src_e = ((y + NY - dy) % NY) * 2 + flip(xh, dx)
                remote(s_ref, s1.at[src_e], s1_send.at[dy * 2 + dx], s1_recv.at[dy * 2 + dx],
                       at(xl, core, y, xh, z)).wait_recv()
    keep_s2 = pltpu.make_async_copy(s1, s_all.at[z, pl.ds(0, 2 * NY)], local_sem.at[3])
    keep_s2.start()
    for dz in range(1, NZ):
        c = remote(s1, s_all.at[z, pl.ds(0, 2 * NY)], s2_send.at[dz], s2_recv.at[dz],
                   at(xl, core, y, xh, (z + dz) % NZ))
        c.start()
        pending.append(c)

    def ring(way, hop, k):
        src_z = (z + (NZ - hop if way == 0 else hop)) % NZ
        to_z = (z + (1 if way == 0 else NZ - 1)) % NZ
        return remote(a_all.at[src_z, k], a_all.at[src_z, k], ring_send.at[way, hop, k],
                      ring_recv.at[way, hop, k], at(xl, core, y, xh, to_z))

    def arrive(way, hop, k):
        src_z = (z + (NZ - 1 - hop if way == 0 else hop + 1)) % NZ
        remote(a_all.at[src_z, k], a_all.at[src_z, k], ring_send.at[way, hop, k],
               ring_recv.at[way, hop, k], at(xl, core, y, xh, z)).wait_recv()

    def carries(way, hop, k):
        return hop < 3 or (k < 2) == (way == 0)

    def launch(way, hop, k):
        c = ring(way, hop, k)
        c.start()
        pending.append(c)

    keep_a.wait()
    for k in range(4):
        for dc in range(2):
            if k or dc:
                remote(
                    a_hbm.at[:, pl.ds(0, depth)],
                    a_all.at[z, k, flip(core, dc)], row_send.at[k * 2 + dc], row_recv.at[k * 2 + dc],
                    at(xl, core, y, xh, z)).wait_recv()
        for way in range(2):
            launch(way, 0, k)

    def event(dist, k):
        for way in range(2):
            if carries(way, dist - 1, k):
                arrive(way, dist - 1, k)
                if dist < 4 and carries(way, dist, k):
                    launch(way, dist, k)

    keep_s2.wait()
    for dz in range(1, NZ):
        remote(s1, s_all.at[(z + NZ - dz) % NZ, pl.ds(0, 2 * NY)], s2_send.at[dz], s2_recv.at[dz],
               at(xl, core, y, xh, z)).wait_recv()
    load_f.wait()

    width = 3 * LANES

    def hankel(pair):
        for yy in range(2):
            base = ((2 * pair + yy) * 2 + xh) * NZ + z
            blocks = []
            for q in range(5):
                b = base + q
                blocks.append(s_all[b % NZ, b // NZ].astype(F32))
            strip = jnp.concatenate(blocks, axis=1)
            span = strip.shape[1]
            for s in range(STRIDE):
                moved = strip if s == 0 else pltpu.roll(strip, span - s, 1)
                for d in range(3):
                    expand[d * 16 + s * STRIDE:d * 16 + (s + 1) * STRIDE, :] = moved[d * STRIDE:(d + 1) * STRIDE, :]

            def one(b, carry):
                turned = pltpu.roll(expand[...], lax.rem(span - STRIDE * b, span), 1).astype(BF)
                for part in range(taps // (16 * 32)):
                    for d in range(3):
                        hank[pl.ds(pl.multiple_of((32 * part + b) * 16, 16), 16),
                             yy * width + d * LANES:yy * width + (d + 1) * LANES] = (
                            turned[d * 16:(d + 1) * 16, part * LANES:(part + 1) * LANES])
                return carry

            lax.fori_loop(0, 32, one, 0)

    def correlate(pair, nb):
        def one(mb, carry):
            r = pl.ds(pl.multiple_of(mb * 512, 512), 512)
            corr[r, pair * 768 + nb * 256:pair * 768 + (nb + 1) * 256] = jnp.dot(
                filt[r, :], hank[:, nb * 256:(nb + 1) * 256], preferred_element_type=F32).astype(BF)
            return carry

        lax.fori_loop(0, filt.shape[0] // 512, one, 0)

    def pieces(t):
        if t == 0:
            return [(z, 0), (z, 2)], [(z, 1), (z, 3)]
        if t == 7:
            far = (z + 4) % NZ
            return [(far, 0), (far, 2)], [(far, 1), (far, 3)]
        dist, kp = (t + 1) // 2, (t + 1) % 2
        lo, hi = (z + NZ - dist) % NZ, (z + dist) % NZ
        return [(lo, 2 * kp), (hi, 2 * kp)], [(lo, 2 * kp + 1), (hi, 2 * kp + 1)]

    def project(t):
        keep, give = pieces(t)
        left = jnp.concatenate(
            [a_all[zs, k, c] for c in (1 - core, core) for zs, k in keep + give], axis=0)

        def one(nb, carry):
            cols = pl.ds(pl.multiple_of(nb * 256, 256), 256)
            part = jnp.dot(left, corr[:, cols], preferred_element_type=F32)
            c1s[t, :, cols] = part[:128].astype(BF)
            own[t, :, cols] = part[128:]
            return carry

        lax.fori_loop(0, corr.shape[1] // 256, one, 0)
        c = remote(c1s.at[t], c1r.at[t], c1_send.at[t], c1_recv.at[t], at(xl, 1 - core, y, xh, z))
        c.start()
        pending.append(c)

    def halve(t):
        remote(c1s.at[t], c1r.at[t], c1_send.at[t], c1_recv.at[t], at(xl, core, y, xh, z)).wait_recv()
        c2s[t] = (own[t, 64:128] + c1r[t, 64:128].astype(F32)).astype(BF)
        c = remote(c2s.at[t], c2r.at[t], c2_send.at[t], c2_recv.at[t], at(1 - xl, core, y, xh, z))
        c.start()
        pending.append(c)
        own[t, 0:64] = own[t, 0:64] + c1r[t, 0:64].astype(F32)

    def out_rows(t, sub, y_src):
        zs, k = pieces(t)[0][sub]
        return pl.ds(pl.multiple_of(((y_src * 2 + flip(xh, k >> 1)) * NZ + zs) * rows, rows), rows)

    def finish(t):
        remote(c2s.at[t], c2r.at[t], c2_send.at[t], c2_recv.at[t], at(xl, core, y, xh, z)).wait_recv()
        done[t] = (own[t, 0:64] + c2r[t].astype(F32)).astype(BF)
        for sub in range(2):
            for dy in range(NY):
                to_y = (y + dy) % NY
                src = done.at[t, pl.ds(sub * rows, rows), pl.ds(pl.multiple_of(to_y * width, LANES), width)]
                dst = out_ref.at[out_rows(t, sub, y)]
                n = (t * 2 + sub) * NY + dy
                if dy == 0:
                    c = pltpu.make_async_copy(src, dst, keep_sem.at[t * 2 + sub])
                    c.start()
                    kept.append(c)
                else:
                    c = remote(src, dst, c3_send.at[n], c3_recv.at[n], at(xl, core, to_y, xh, z))
                    c.start()
                    pending.append(c)

    kept = []
    hankel(0)
    event(1, 0)
    correlate(0, 0)
    correlate(0, 1)
    event(1, 1)
    correlate(0, 2)
    hankel(1)
    event(1, 2)
    correlate(1, 0)
    correlate(1, 1)
    event(1, 3)
    correlate(1, 2)
    project(0)
    event(2, 0)
    project(1)
    halve(0)
    project(2)
    event(2, 1)
    halve(1)
    project(3)
    halve(2)
    event(2, 2)
    finish(0)
    halve(3)
    event(2, 3)
    project(4)
    event(3, 0)
    halve(4)
    finish(1)
    event(3, 1)
    project(5)
    event(3, 2)
    halve(5)
    finish(2)
    event(3, 3)
    project(6)
    event(4, 0)
    event(4, 2)
    halve(6)
    finish(3)
    event(4, 1)
    event(4, 3)
    project(7)
    finish(4)
    halve(7)
    finish(5)
    finish(6)
    finish(7)

    for t in range(8):
        for sub in range(2):
            for dy in range(1, NY):
                n = (t * 2 + sub) * NY + dy
                src_y = (y + NY - dy) % NY
                remote(done.at[t, pl.ds(sub * rows, rows), pl.ds(0, width)], out_ref.at[out_rows(t, sub, src_y)],
                       c3_send.at[n], c3_recv.at[n], at(xl, core, y, xh, z)).wait_recv()
    for c in pending:
        c.wait_send()
    for c in kept:
        c.wait()


def shards(strain, basis_filters, coefficients):
    detectors, block_len = strain.shape
    filters_here, taps = basis_filters.shape
    rows, _ = coefficients.shape
    phases = strain.reshape(detectors, block_len // STRIDE, STRIDE).transpose(0, 2, 1)
    phases = jnp.pad(phases.reshape(detectors * STRIDE, block_len // STRIDE), ((0, 16 - detectors * STRIDE), (0, 0)))
    width = detectors * LANES
    cols = NY * width
    out_rows = rows * 64
    dma = pltpu.SemaphoreType.DMA
    out = pl.pallas_call(
        kernel,
        out_shape=jax.ShapeDtypeStruct((out_rows, width), BF),
        in_specs=[
            pl.BlockSpec(memory_space=pltpu.VMEM),
            pl.BlockSpec(memory_space=pl.ANY),
            pl.BlockSpec(memory_space=pl.ANY),
        ],
        out_specs=pl.BlockSpec(memory_space=pltpu.VMEM),
        scratch_shapes=[
            pltpu.VMEM((NZ, 4, 2, rows, filters_here), BF),
            pltpu.VMEM((2 * NY, 16, LANES), BF),
            pltpu.VMEM((NZ, 2 * NY + 1, 16, LANES), BF),
            pltpu.VMEM((filters_here, taps), BF),
            pltpu.VMEM((taps, 2 * width), BF),
            pltpu.VMEM((48, 5 * LANES), F32),
            pltpu.VMEM((filters_here, cols), BF),
            pltpu.VMEM((8, 128, cols), BF),
            pltpu.VMEM((8, 128, cols), BF),
            pltpu.VMEM((8, 128, cols), F32),
            pltpu.VMEM((8, 64, cols), BF),
            pltpu.VMEM((8, 64, cols), BF),
            pltpu.VMEM((8, 64, cols), BF),
            dma((4,)),
            dma((8,)), dma((8,)), dma((8,)), dma((8,)), dma((8,)), dma((8,)),
            dma((2, 4, 4)), dma((2, 4, 4)),
            dma((8,)), dma((8,)), dma((8,)), dma((8,)),
            dma((64,)), dma((64,)), dma((16,)),
        ],
        compiler_params=pltpu.CompilerParams(
            collective_id=0, has_side_effects=True, vmem_limit_bytes=60 * 1024 * 1024),
    )(phases, basis_filters, coefficients)
    return out.reshape(out_rows, detectors, LANES)


def solution(mesh):
    placed = (P(None, "tm"), P("basis", None), P(("basis", "tm"), None))
    return jax.shard_map(
        shards, mesh=mesh, in_specs=placed, out_specs=P("basis", None, "tm"), check_vma=False
    )
```

profile of v0, /device:TPU:1, one launch (start us, length us, event | category | flops | bytes accessed | tf_op | source)
XLA Modules:
  0.0 98.5 jit_solution(8104697398256251744)
XLA Ops:
  0.0 0.9 reshape.9
  0.9 0.1 copy.6
  1.0 0.6 pad.4.s_ref
  1.6 93.6 %shard_map.37 = bf16[2048,384]{1,0:T(8,128)(2,1)} custom-call(bf16[16,128]{1,0:T(8,128)(2,1)} %pad.4.s_ref, bf16[1024,2048]{1,0:T(8,128)(2,1)} %f_hbm.1, bf16[32,4096]{1,0:T(8,128)(2,1)} %a_hbm.1), custom_call_target="tpu_custom_call" | custom-call | tf_op jit(solution)/shard_map/pallas_call | solution.py:309
  95.2 1.7 %copy.7 = bf16[2048,384]{0,1:T(8,128)(2,1)S(1)} copy(bf16[2048,384]{1,0:T(8,128)(2,1)} %shard_map.37) | data formatting | bytes 3145728 | tf_op jit(solution)/shard_map/pallas_call | solution.py:309
  97.0 1.6 %copy.8 = bf16[2048,3,128]{2,0,1:T(8,128)(2,1)} copy(bf16[2048,3,128]{0,2,1:T(8,128)(2,1)S(1)} %bitcast.2) | data formatting | bytes 3145728 | tf_op jit(solution)/shard_map/reshape | solution.py:341
  (1 shorter events, 0.0 us)
where the time goes:
time: 98.8 us; the launch traced here: 98.5 us
  Pallas kernels  93.6 us (95%)
  local copies, waits for them, and re-layouts  4.91 us (5%)
    pallas_call x1, Pallas kernels, shards(): pl.pallas_call(kernel, out_shape=jax.ShapeDtypeStruct((out_rows, width),...  93.6 us

commit v1 on v0

--- a/solution.py
+++ b/solution.py
@@ -14,7 +14,7 @@
 
 def kernel(
     s_ref, f_hbm, a_hbm, out_ref,
-    a_all, s1, s_all, filt, hank, expand, corr, c1s, c1r, own, c2s, c2r, done,
+    a_all, s1, s_next, filt, hank, expand, corr, c1s, c1r, own, c2s, c2r, done,
     local_sem, s1_send, s1_recv, s2_send, s2_recv, row_send, row_recv,
     ring_send, ring_recv, c1_send, c1_recv, c2_send, c2_recv, c3_send, c3_recv, keep_sem,
 ):
@@ -59,16 +59,16 @@
         a_hbm.at[:, pl.ds(pl.multiple_of(i * depth, LANES), depth)], a_all.at[z, 0, core], local_sem.at[1]
     )
     keep_a.start()
-    keep_s = pltpu.make_async_copy(s_ref, s1.at[e], local_sem.at[2])
+    keep_s = pltpu.make_async_copy(s_ref, s1.at[y, xh], local_sem.at[2])
     keep_s.start()
-    s_all[:, 2 * NY] = jnp.zeros((NZ,) + s_ref.shape, BF)
+    s1[NY] = jnp.zeros((2,) + s_ref.shape, BF)
     pl.semaphore_wait(barrier, len(peers))
 
     pending = []
     for dy in range(NY):
         for dx in range(2):
             if dy or dx:
-                c = remote(s_ref, s1.at[e], s1_send.at[dy * 2 + dx], s1_recv.at[dy * 2 + dx],
+                c = remote(s_ref, s1.at[y, xh], s1_send.at[dy * 2 + dx], s1_recv.at[dy * 2 + dx],
                            at(xl, core, (y + dy) % NY, flip(xh, dx), z))
                 c.start()
                 pending.append(c)
@@ -82,21 +82,6 @@
                     at(txl, tcore, y, txh, z))
                 c.start()
                 pending.append(c)
-    keep_s.wait()
-    for dy in range(NY):
-        for dx in range(2):
-            if dy or dx:
-                src_e = ((y + NY - dy) % NY) * 2 + flip(xh, dx)
-                remote(s_ref, s1.at[src_e], s1_send.at[dy * 2 + dx], s1_recv.at[dy * 2 + dx],
-                       at(xl, core, y, xh, z)).wait_recv()
-    keep_s2 = pltpu.make_async_copy(s1, s_all.at[z, pl.ds(0, 2 * NY)], local_sem.at[3])
-    keep_s2.start()
-    for dz in range(1, NZ):
-        c = remote(s1, s_all.at[z, pl.ds(0, 2 * NY)], s2_send.at[dz], s2_recv.at[dz],
-                   at(xl, core, y, xh, (z + dz) % NZ))
-        c.start()
-        pending.append(c)
-
     def ring(way, hop, k):
         src_z = (z + (NZ - hop if way == 0 else hop)) % NZ
         to_z = (z + (1 if way == 0 else NZ - 1)) % NZ
@@ -126,6 +111,19 @@
                     at(xl, core, y, xh, z)).wait_recv()
         for way in range(2):
             launch(way, 0, k)
+        if k == 0:
+            keep_s.wait()
+            for dy in range(NY):
+                for dx in range(2):
+                    if dy or dx:
+                        remote(s_ref, s1.at[(y + NY - dy) % NY, flip(xh, dx)], s1_send.at[dy * 2 + dx],
+                               s1_recv.at[dy * 2 + dx], at(xl, core, y, xh, z)).wait_recv()
+            for q in range(1, 5):
+                m = xh + (NZ + q - 1 - z) // NZ
+                c = remote(s1.at[pl.ds(m // 2, NY), m % 2], s_next.at[q - 1], s2_send.at[q], s2_recv.at[q],
+                           at(xl, core, y, xh, (z + NZ - q) % NZ))
+                c.start()
+                pending.append(c)
 
     def event(dist, k):
         for way in range(2):
@@ -134,21 +132,21 @@
                 if dist < 4 and carries(way, dist, k):
                     launch(way, dist, k)
 
-    keep_s2.wait()
-    for dz in range(1, NZ):
-        remote(s1, s_all.at[(z + NZ - dz) % NZ, pl.ds(0, 2 * NY)], s2_send.at[dz], s2_recv.at[dz],
+    event(1, 0)
+    for q in range(1, 5):
+        remote(s1.at[pl.ds(0, NY), 0], s_next.at[q - 1], s2_send.at[q], s2_recv.at[q],
                at(xl, core, y, xh, z)).wait_recv()
+    event(1, 1)
     load_f.wait()
 
     width = 3 * LANES
 
     def hankel(pair):
         for yy in range(2):
-            base = ((2 * pair + yy) * 2 + xh) * NZ + z
-            blocks = []
-            for q in range(5):
-                b = base + q
-                blocks.append(s_all[b % NZ, b // NZ].astype(F32))
+            ya = (y + 2 * pair + yy) % NY
+            blocks = [s1[ya, xh].astype(F32)]
+            for q in range(4):
+                blocks.append(s_next[q, ya].astype(F32))
             strip = jnp.concatenate(blocks, axis=1)
             span = strip.shape[1]
             for s in range(STRIDE):
@@ -186,42 +184,58 @@
         lo, hi = (z + NZ - dist) % NZ, (z + dist) % NZ
         return [(lo, 2 * kp), (hi, 2 * kp)], [(lo, 2 * kp + 1), (hi, 2 * kp + 1)]
 
-    def project(t):
+    half = 2 * width
+
+    def span_of(p):
+        return pl.ds(p * half, half)
+
+    def first(t, p):
+        u = t * 2 + p
+        cut = (t, slice(None), span_of(p))
+        return remote(c1s.at[cut], c1r.at[cut], c1_send.at[u], c1_recv.at[u], at(xl, 1 - core, y, xh, z))
+
+    def second(t, p):
+        u = t * 2 + p
+        cut = (t, slice(None), span_of(p))
+        return remote(c2s.at[cut], c2r.at[cut], c2_send.at[u], c2_recv.at[u], at(1 - xl, core, y, xh, z))
+
+    def project(t, p):
         keep, give = pieces(t)
         left = jnp.concatenate(
             [a_all[zs, k, c] for c in (1 - core, core) for zs, k in keep + give], axis=0)
 
         def one(nb, carry):
-            cols = pl.ds(pl.multiple_of(nb * 256, 256), 256)
+            cols = pl.ds(pl.multiple_of(p * half + nb * 256, 256), 256)
             part = jnp.dot(left, corr[:, cols], preferred_element_type=F32)
             c1s[t, :, cols] = part[:128].astype(BF)
             own[t, :, cols] = part[128:]
             return carry
 
-        lax.fori_loop(0, corr.shape[1] // 256, one, 0)
-        c = remote(c1s.at[t], c1r.at[t], c1_send.at[t], c1_recv.at[t], at(xl, 1 - core, y, xh, z))
+        lax.fori_loop(0, half // 256, one, 0)
+        c = first(t, p)
         c.start()
         pending.append(c)
 
-    def halve(t):
-        remote(c1s.at[t], c1r.at[t], c1_send.at[t], c1_recv.at[t], at(xl, core, y, xh, z)).wait_recv()
-        c2s[t] = (own[t, 64:128] + c1r[t, 64:128].astype(F32)).astype(BF)
-        c = remote(c2s.at[t], c2r.at[t], c2_send.at[t], c2_recv.at[t], at(1 - xl, core, y, xh, z))
+    def halve(t, p):
+        first(t, p).wait_recv()
+        cols = span_of(p)
+        c2s[t, :, cols] = (own[t, 64:128, cols] + c1r[t, 64:128, cols].astype(F32)).astype(BF)
+        c = second(t, p)
         c.start()
         pending.append(c)
-        own[t, 0:64] = own[t, 0:64] + c1r[t, 0:64].astype(F32)
+        own[t, 0:64, cols] = own[t, 0:64, cols] + c1r[t, 0:64, cols].astype(F32)
 
     def out_rows(t, sub, y_src):
         zs, k = pieces(t)[0][sub]
         return pl.ds(pl.multiple_of(((y_src * 2 + flip(xh, k >> 1)) * NZ + zs) * rows, rows), rows)
 
-    def finish(t):
-        remote(c2s.at[t], c2r.at[t], c2_send.at[t], c2_recv.at[t], at(xl, core, y, xh, z)).wait_recv()
-        done[t] = (own[t, 0:64] + c2r[t].astype(F32)).astype(BF)
+    def finish(t, p):
+        second(t, p).wait_recv()
+        cols = span_of(p)
+        done[t, :, cols] = (own[t, 0:64, cols] + c2r[t, :, cols].astype(F32)).astype(BF)
         for sub in range(2):
-            for dy in range(NY):
-                to_y = (y + dy) % NY
-                src = done.at[t, pl.ds(sub * rows, rows), pl.ds(pl.multiple_of(to_y * width, LANES), width)]
+            for dy in (2 * p, 2 * p + 1):
+                src = done.at[t, pl.ds(sub * rows, rows), pl.ds(dy * width, width)]
                 dst = out_ref.at[out_rows(t, sub, y)]
                 n = (t * 2 + sub) * NY + dy
                 if dy == 0:
@@ -229,59 +243,77 @@
                     c.start()
                     kept.append(c)
                 else:
-                    c = remote(src, dst, c3_send.at[n], c3_recv.at[n], at(xl, core, to_y, xh, z))
+                    c = remote(src, dst, c3_send.at[n], c3_recv.at[n], at(xl, core, (y + dy) % NY, xh, z))
                     c.start()
                     pending.append(c)
 
     kept = []
-    hankel(0)
-    event(1, 0)
-    correlate(0, 0)
-    correlate(0, 1)
-    event(1, 1)
-    correlate(0, 2)
     hankel(1)
     event(1, 2)
+    event(1, 3)
     correlate(1, 0)
+    event(2, 0)
     correlate(1, 1)
-    event(1, 3)
+    event(2, 1)
     correlate(1, 2)
-    project(0)
-    event(2, 0)
-    project(1)
-    halve(0)
-    project(2)
-    event(2, 1)
-    halve(1)
-    project(3)
-    halve(2)
+    project(0, 1)
+    project(1, 1)
+    halve(0, 1)
     event(2, 2)
-    finish(0)
-    halve(3)
+    project(2, 1)
+    halve(1, 1)
+    project(3, 1)
+    halve(2, 1)
     event(2, 3)
-    project(4)
+    project(4, 1)
+    halve(3, 1)
+    hankel(0)
+    halve(4, 1)
     event(3, 0)
-    halve(4)
-    finish(1)
     event(3, 1)
-    project(5)
+    finish(0, 1)
+    correlate(0, 0)
     event(3, 2)
-    halve(5)
-    finish(2)
+    project(5, 1)
+    finish(1, 1)
+    correlate(0, 1)
+    halve(5, 1)
     event(3, 3)
-    project(6)
-    event(4, 0)
-    event(4, 2)
-    halve(6)
-    finish(3)
-    event(4, 1)
-    event(4, 3)
-    project(7)
-    finish(4)
-    halve(7)
-    finish(5)
-    finish(6)
-    finish(7)
+    finish(2, 1)
+    project(6, 1)
+    correlate(0, 2)
+    halve(6, 1)
+    finish(3, 1)
+    project(0, 0)
+    project(1, 0)
+    halve(0, 0)
+    finish(4, 1)
+    project(2, 0)
+    halve(1, 0)
+    project(3, 0)
+    halve(2, 0)
+    finish(5, 1)
+    for k in range(4):
+        event(4, k)
+    project(7, 1)
+    halve(3, 0)
+    project(4, 0)
+    halve(7, 1)
+    finish(6, 1)
+    project(5, 0)
+    halve(4, 0)
+    finish(0, 0)
+    project(6, 0)
+    halve(5, 0)
+    finish(1, 0)
+    project(7, 0)
+    halve(6, 0)
+    finish(2, 0)
+    halve(7, 0)
+    finish(3, 0)
+    finish(7, 1)
+    for t in range(4, 8):
+        finish(t, 0)
 
     for t in range(8):
         for sub in range(2):
@@ -317,8 +349,8 @@
         out_specs=pl.BlockSpec(memory_space=pltpu.VMEM),
         scratch_shapes=[
             pltpu.VMEM((NZ, 4, 2, rows, filters_here), BF),
-            pltpu.VMEM((2 * NY, 16, LANES), BF),
-            pltpu.VMEM((NZ, 2 * NY + 1, 16, LANES), BF),
+            pltpu.VMEM((NY + 1, 2, 16, LANES), BF),
+            pltpu.VMEM((4, NY, 16, LANES), BF),
             pltpu.VMEM((filters_here, taps), BF),
             pltpu.VMEM((taps, 2 * width), BF),
             pltpu.VMEM((48, 5 * LANES), F32),
@@ -332,7 +364,7 @@
             dma((4,)),
             dma((8,)), dma((8,)), dma((8,)), dma((8,)), dma((8,)), dma((8,)),
             dma((2, 4, 4)), dma((2, 4, 4)),
-            dma((8,)), dma((8,)), dma((8,)), dma((8,)),
+            dma((16,)), dma((16,)), dma((16,)), dma((16,)),
             dma((64,)), dma((64,)), dma((16,)),
         ],
         compiler_params=pltpu.CompilerParams(

time: 98.8 us -> 90.3 us (0.914)
  Pallas kernels: 93.6 us -> 85.2 us
    pallas_call x1, Pallas kernels: 93.6 us -> 85.2 us  [shards(): pl.pallas_call(kernel, out_shape=jax.ShapeDtypeStruct((out_rows, width),...]
where the time goes in v1:
time: 90.3 us; the launch traced here: 90.1 us
  Pallas kernels  85.2 us (94%)
  local copies, waits for them, and re-layouts  4.91 us (5%)
    pallas_call x1, Pallas kernels, shards(): pl.pallas_call(kernel, out_shape=jax.ShapeDtypeStruct((out_rows, width),...  85.2 us

profile of v1, /device:TPU:1, one launch (start us, length us, event | category | flops | bytes accessed | tf_op | source)
XLA Modules:
  0.0 90.1 jit_solution(9001889733110129305)
XLA Ops:
  0.0 0.9 %reshape.9 = bf16[3,128,4]{2,1,0:T(8,128)(2,1)S(1)} reshape(bf16[3,512]{1,0:T(4,128)(2,1)} %param.3) | data formatting | bytes 6144 | tf_op jit(solution)/shard_map/reshape | solution.py:335
  0.9 0.1 copy.6
  1.0 0.6 pad.4.s_ref
  1.6 85.2 %shard_map.37 = bf16[2048,384]{1,0:T(8,128)(2,1)} custom-call(bf16[16,128]{1,0:T(8,128)(2,1)} %pad.4.s_ref, bf16[1024,2048]{1,0:T(8,128)(2,1)} %f_hbm.1, bf16[32,4096]{1,0:T(8,128)(2,1)} %a_hbm.1), custom_call_target="tpu_custom_call" | custom-call | tf_op jit(solution)/shard_map/pallas_call | solution.py:341
  86.8 1.7 %copy.7 = bf16[2048,384]{0,1:T(8,128)(2,1)S(1)} copy(bf16[2048,384]{1,0:T(8,128)(2,1)} %shard_map.37) | data formatting | bytes 3145728 | tf_op jit(solution)/shard_map/pallas_call | solution.py:341
  88.5 1.6 %copy.8 = bf16[2048,3,128]{2,0,1:T(8,128)(2,1)} copy(bf16[2048,3,128]{0,2,1:T(8,128)(2,1)S(1)} %bitcast.2) | data formatting | bytes 3145728 | tf_op jit(solution)/shard_map/reshape | solution.py:373
  (1 shorter events, 0.0 us)

commit v2 on v1

--- a/solution.py
+++ b/solution.py
@@ -154,16 +154,17 @@
                 for d in range(3):
                     expand[d * 16 + s * STRIDE:d * 16 + (s + 1) * STRIDE, :] = moved[d * STRIDE:(d + 1) * STRIDE, :]
 
-            def one(b, carry):
-                turned = pltpu.roll(expand[...], lax.rem(span - STRIDE * b, span), 1).astype(BF)
-                for part in range(taps // (16 * 32)):
-                    for d in range(3):
-                        hank[pl.ds(pl.multiple_of((32 * part + b) * 16, 16), 16),
-                             yy * width + d * LANES:yy * width + (d + 1) * LANES] = (
-                            turned[d * 16:(d + 1) * 16, part * LANES:(part + 1) * LANES])
-                return carry
-
-            lax.fori_loop(0, 32, one, 0)
+            def one(g, moving):
+                for b in range(4):
+                    turned = (moving if b == 0 else pltpu.roll(moving, span - STRIDE * b, 1)).astype(BF)
+                    for part in range(taps // (16 * 32)):
+                        for d in range(3):
+                            hank[pl.ds(pl.multiple_of((32 * part + 4 * g + b) * 16, 16), 16),
+                                 yy * width + d * LANES:yy * width + (d + 1) * LANES] = (
+                                turned[d * 16:(d + 1) * 16, part * LANES:(part + 1) * LANES])
+                return pltpu.roll(moving, span - 4 * STRIDE, 1)
+
+            lax.fori_loop(0, 8, one, expand[...])
 
     def correlate(pair, nb):
         def one(mb, carry):
@@ -204,14 +205,10 @@
         left = jnp.concatenate(
             [a_all[zs, k, c] for c in (1 - core, core) for zs, k in keep + give], axis=0)
 
-        def one(nb, carry):
-            cols = pl.ds(pl.multiple_of(p * half + nb * 256, 256), 256)
-            part = jnp.dot(left, corr[:, cols], preferred_element_type=F32)
-            c1s[t, :, cols] = part[:128].astype(BF)
-            own[t, :, cols] = part[128:]
-            return carry
-
-        lax.fori_loop(0, half // 256, one, 0)
+        cols = span_of(p)
+        part = jnp.dot(left, corr[:, cols], preferred_element_type=F32)
+        c1s[t, :, cols] = part[:128].astype(BF)
+        own[t, :, cols] = part[128:]
         c = first(t, p)
         c.start()
         pending.append(c)
@@ -231,12 +228,14 @@
 
     def finish(t, p):
         second(t, p).wait_recv()
-        cols = span_of(p)
-        done[t, :, cols] = (own[t, 0:64, cols] + c2r[t, :, cols].astype(F32)).astype(BF)
+        for dy in (2 * p, 2 * p + 1):
+            for d in range(3):
+                at_ = pl.ds(dy * width + d * LANES, LANES)
+                done[t, dy, d] = (own[t, 0:64, at_] + c2r[t, :, at_].astype(F32)).astype(BF)
         for sub in range(2):
             for dy in (2 * p, 2 * p + 1):
-                src = done.at[t, pl.ds(sub * rows, rows), pl.ds(dy * width, width)]
-                dst = out_ref.at[out_rows(t, sub, y)]
+                src = done.at[t, dy, :, pl.ds(sub * rows, rows)]
+                dst = out_ref.at[:, out_rows(t, sub, y)]
                 n = (t * 2 + sub) * NY + dy
                 if dy == 0:
                     c = pltpu.make_async_copy(src, dst, keep_sem.at[t * 2 + sub])
@@ -320,7 +319,7 @@
             for dy in range(1, NY):
                 n = (t * 2 + sub) * NY + dy
                 src_y = (y + NY - dy) % NY
-                remote(done.at[t, pl.ds(sub * rows, rows), pl.ds(0, width)], out_ref.at[out_rows(t, sub, src_y)],
+                remote(done.at[t, dy, :, pl.ds(sub * rows, rows)], out_ref.at[:, out_rows(t, sub, src_y)],
                        c3_send.at[n], c3_recv.at[n], at(xl, core, y, xh, z)).wait_recv()
     for c in pending:
         c.wait_send()
@@ -340,7 +339,7 @@
     dma = pltpu.SemaphoreType.DMA
     out = pl.pallas_call(
         kernel,
-        out_shape=jax.ShapeDtypeStruct((out_rows, width), BF),
+        out_shape=jax.ShapeDtypeStruct((detectors, out_rows, LANES), BF),
         in_specs=[
             pl.BlockSpec(memory_space=pltpu.VMEM),
             pl.BlockSpec(memory_space=pl.ANY),
@@ -360,7 +359,7 @@
             pltpu.VMEM((8, 128, cols), F32),
             pltpu.VMEM((8, 64, cols), BF),
             pltpu.VMEM((8, 64, cols), BF),
-            pltpu.VMEM((8, 64, cols), BF),
+            pltpu.VMEM((8, NY, detectors, 64, LANES), BF),
             dma((4,)),
             dma((8,)), dma((8,)), dma((8,)), dma((8,)), dma((8,)), dma((8,)),
             dma((2, 4, 4)), dma((2, 4, 4)),
@@ -370,7 +369,7 @@
         compiler_params=pltpu.CompilerParams(
             collective_id=0, has_side_effects=True, vmem_limit_bytes=60 * 1024 * 1024),
     )(phases, basis_filters, coefficients)
-    return out.reshape(out_rows, detectors, LANES)
+    return out.transpose(1, 0, 2)
 
 
 def solution(mesh):

time: 90.3 us -> 87.8 us (0.972)
  Pallas kernels: 85.2 us -> 83.3 us
    unnamed x0 -> x1, local copies, waits for them, and re-layouts: none -> 2.65 us
    pallas_call x1, Pallas kernels: 85.2 us -> 83.3 us  [shards(): pl.pallas_call(kernel, out_shape=jax.ShapeDtypeStruct((detectors, out_row...]
    pallas_call x1 -> x0, local copies, waits for them, and re-layouts: 1.71 us -> none  [shards(): pl.pallas_call(kernel, out_shape=jax.ShapeDtypeStruct((out_rows, width),...]
    reshape x1 -> x0, local copies, waits for them, and re-layouts: 1.57 us -> none  [shards(): return out.reshape(out_rows, detectors, LANES)]
where the time goes in v2:
time: 87.8 us; the launch traced here: 87.6 us
  Pallas kernels  83.3 us (95%)
  local copies, waits for them, and re-layouts  4.28 us (5%)
    pallas_call x1, Pallas kernels, shards(): pl.pallas_call(kernel, out_shape=jax.ShapeDtypeStruct((detectors, out_row...  83.3 us
    unnamed x1, local copies, waits for them, and re-layouts  2.65 us

profile of v2, /device:TPU:1, one launch (start us, length us, event | category | flops | bytes accessed | tf_op | source)
XLA Modules:
  0.0 87.6 jit_solution(3078935013486540981)
XLA Ops:
  0.0 0.9 %reshape.6 = bf16[3,128,4]{2,1,0:T(8,128)(2,1)S(1)} reshape(bf16[3,512]{1,0:T(4,128)(2,1)} %param.3) | data formatting | bytes 6144 | tf_op jit(solution)/shard_map/reshape | solution.py:334
  0.9 0.1 copy.5
  1.0 0.6 pad.4.s_ref
  1.6 83.3 %shard_map.37 = bf16[3,2048,128]{2,1,0:T(8,128)(2,1)} custom-call(bf16[16,128]{1,0:T(8,128)(2,1)} %pad.4.s_ref, bf16[1024,2048]{1,0:T(8,128)(2,1)} %f_hbm.1, bf16[32,4096]{1,0:T(8,128)(2,1)} %a_hbm.1), custom_call_target="tpu_custom_call" | custom-call | tf_op jit(solution)/shard_map/pallas_call | solution.py:340
  85.0 2.7 %copy.7 = bf16[2048,3,128]{2,0,1:T(8,128)(2,1)} copy(bf16[2048,3,128]{2,0,1:T(8,128)(2,1)} %bitcast.2) | data formatting | bytes 3145728
  (1 shorter events, 0.0 us)

commit v3 on v2

--- a/solution.py
+++ b/solution.py
@@ -248,71 +248,75 @@
 
     kept = []
     hankel(1)
+    correlate(1, 0)
     event(1, 2)
+    correlate(1, 1)
+    correlate(1, 2)
     event(1, 3)
-    correlate(1, 0)
-    event(2, 0)
-    correlate(1, 1)
-    event(2, 1)
-    correlate(1, 2)
     project(0, 1)
     project(1, 1)
     halve(0, 1)
-    event(2, 2)
     project(2, 1)
     halve(1, 1)
+    event(2, 0)
+    hankel(0)
+    halve(2, 1)
+    correlate(0, 0)
+    event(2, 1)
     project(3, 1)
-    halve(2, 1)
-    event(2, 3)
-    project(4, 1)
+    correlate(0, 1)
     halve(3, 1)
-    hankel(0)
-    halve(4, 1)
-    event(3, 0)
-    event(3, 1)
     finish(0, 1)
-    correlate(0, 0)
-    event(3, 2)
-    project(5, 1)
-    finish(1, 1)
-    correlate(0, 1)
-    halve(5, 1)
-    event(3, 3)
-    finish(2, 1)
-    project(6, 1)
     correlate(0, 2)
-    halve(6, 1)
-    finish(3, 1)
     project(0, 0)
     project(1, 0)
     halve(0, 0)
-    finish(4, 1)
+    event(2, 2)
     project(2, 0)
     halve(1, 0)
+    finish(1, 1)
     project(3, 0)
     halve(2, 0)
+    finish(2, 1)
+    halve(3, 0)
+    event(2, 3)
+    project(4, 1)
+    project(4, 0)
+    halve(4, 1)
+    event(3, 0)
+    halve(4, 0)
+    finish(3, 1)
+    finish(0, 0)
+    event(3, 1)
+    project(5, 1)
+    project(5, 0)
+    halve(5, 1)
+    finish(1, 0)
+    finish(2, 0)
+    halve(5, 0)
+    event(3, 2)
+    finish(4, 1)
+    finish(3, 0)
+    event(3, 3)
+    project(6, 1)
+    project(6, 0)
+    halve(6, 1)
+    halve(6, 0)
+    finish(4, 0)
     finish(5, 1)
-    for k in range(4):
-        event(4, k)
+    finish(5, 0)
+    event(4, 0)
+    event(4, 1)
+    event(4, 2)
+    event(4, 3)
     project(7, 1)
-    halve(3, 0)
-    project(4, 0)
+    project(7, 0)
     halve(7, 1)
     finish(6, 1)
-    project(5, 0)
-    halve(4, 0)
-    finish(0, 0)
-    project(6, 0)
-    halve(5, 0)
-    finish(1, 0)
-    project(7, 0)
-    halve(6, 0)
-    finish(2, 0)
     halve(7, 0)
-    finish(3, 0)
+    finish(6, 0)
     finish(7, 1)
-    for t in range(4, 8):
-        finish(t, 0)
+    finish(7, 0)
 
     for t in range(8):
         for sub in range(2):

time: 87.8 us -> 81.4 us (0.927)
  Pallas kernels: 83.3 us -> 77 us
    pallas_call x1, Pallas kernels: 83.3 us -> 77 us  [shards(): pl.pallas_call(kernel, out_shape=jax.ShapeDtypeStruct((detectors, out_row...]
where the time goes in v3:
time: 81.4 us; the launch traced here: 81.3 us
  Pallas kernels  77 us (95%)
  local copies, waits for them, and re-layouts  4.28 us (5%)
    pallas_call x1, Pallas kernels, shards(): pl.pallas_call(kernel, out_shape=jax.ShapeDtypeStruct((detectors, out_row...  77 us
    unnamed x1, local copies, waits for them, and re-layouts  2.65 us

profile of v3, /device:TPU:1, one launch (start us, length us, event | category | flops | bytes accessed | tf_op | source)
XLA Modules:
  0.0 81.3 jit_solution(17866038578023787269)
XLA Ops:
  0.0 0.9 %reshape.6 = bf16[3,128,4]{2,1,0:T(8,128)(2,1)S(1)} reshape(bf16[3,512]{1,0:T(4,128)(2,1)} %param.3) | data formatting | bytes 6144 | tf_op jit(solution)/shard_map/reshape | solution.py:338
  0.9 0.1 copy.5
  1.0 0.6 pad.4.s_ref
  1.6 77.0 %shard_map.37 = bf16[3,2048,128]{2,1,0:T(8,128)(2,1)} custom-call(bf16[16,128]{1,0:T(8,128)(2,1)} %pad.4.s_ref, bf16[1024,2048]{1,0:T(8,128)(2,1)} %f_hbm.1, bf16[32,4096]{1,0:T(8,128)(2,1)} %a_hbm.1), custom_call_target="tpu_custom_call" | custom-call | tf_op jit(solution)/shard_map/pallas_call | solution.py:344
  78.6 2.7 %copy.7 = bf16[2048,3,128]{2,0,1:T(8,128)(2,1)} copy(bf16[2048,3,128]{2,0,1:T(8,128)(2,1)} %bitcast.2) | data formatting | bytes 3145728
  (1 shorter events, 0.0 us)
